TPU v7x, 256 devices: a whole 4x4x8 slice. The times are simulated.
256 devices in a mesh: seq: 8 (over z_lo, y), outer: 8 (over x, core), inner: 4 (over z_hi).
Axes of the slice: x: 4, y: 4, z: 8 (z_hi: 4, z_lo: 2; z = z_hi * 2 + z_lo), core: 2. Of those that a mesh axis runs over, the one named last changes fastest.
Arguments:
- tokens: bfloat16 [32768, 4096], P(('seq', 'outer', 'inner')), parts along dimension 0, may hold values from -6 to 6
- att_ids: int32 [32768, 2, 2], P(('seq', 'outer', 'inner')), parts along dimension 0, may hold values from 0 to 3, all different within a row
- mlp_ids: int32 [32768, 8], P(('seq', 'outer', 'inner')), parts along dimension 0, may hold values from 0 to 63, all different within a row; in each aligned block of 128 rows (0 to 127, 128 to 255, ...) at most 20 rows name the same one
- att_gain: float32 [4096], replicated, may hold values from 0.25 to 1.75
- att_in: bfloat16 [4096, 768], P('inner'), may hold values from -16 to 16
- att_router: bfloat16 [4096, 8], P('inner'), may hold values from -0.09375 to 0.09375
- att_out: bfloat16 [512, 4096], P(None, 'inner'), may hold values from -0.75 to 0.75
- mlp_gain: float32 [4096], replicated, may hold values from 0.25 to 1.75
- mlp_router: bfloat16 [4096, 64], replicated, may hold values from -0.09375 to 0.09375
- w_up: bfloat16 [64, 4096, 256], P(('outer', 'inner')), may hold values from -0.09375 to 0.09375
- w_down: bfloat16 [64, 256, 4096], P(('outer', 'inner')), may hold values from -0.375 to 0.375
Outputs:
- layer_out: bfloat16 [32768, 4096], P(('seq', 'outer', 'inner')), parts along dimension 0
There are 8 independent parts, one for each index of `seq`. A program takes and returns all parts, laid end to end along the dimension named above; an argument that names none is the same for every part. Nothing has to cross between parts.
Inputs may be any that keep to these rules, and one draw needn't show every extreme that they name: `att_ids`: the 2 ids of one token and head differ. `mlp_ids`: among the rows of one device each expert is named at most 20 times, a bound that some block reaches in some devices' rows.
All inputs are finite; a program needn't handle non-finite values.
Results may differ from a plain program's by a relative error of at most 0.008.
Values may be sent and summed in bfloat16 or wider, within the bound.
A program may use at most 128 MiB of HBM per device.

v0:
```python
import jax
import jax.numpy as jnp
from jax import lax
from jax.sharding import PartitionSpec as P

D = 4096
HEADS = 2
HDIM = 64
ATT_EXP = 4
MLP_TOP = 8
epsilon = 1e-05


def rms_norm(values_in, gain_vector):
    floats = values_in.astype(jnp.float32)
    return (
        floats
        * lax.rsqrt(jnp.mean(floats * floats, axis=-1, keepdims=True) + epsilon)
        * gain_vector
    )


def on_device(
    tokens,
    att_ids,
    mlp_ids,
    att_gain,
    att_in,
    att_router,
    att_out,
    mlp_gain,
    mlp_router,
    w_up,
    w_down,
):
    row_count = tokens.shape[0]
    head_width = HEADS * HDIM
    normed = rms_norm(tokens, att_gain).astype(jnp.bfloat16)
    proj = jnp.dot(
        normed,
        lax.all_gather(att_in, "inner", axis=0, tiled=True),
        preferred_element_type=jnp.float32,
    )
    att_logit = jnp.dot(
        normed,
        lax.all_gather(att_router, "inner", axis=0, tiled=True),
        preferred_element_type=jnp.float32,
    )
    query = proj[:, :head_width].astype(jnp.bfloat16).reshape(row_count, HEADS, HDIM)
    keys = proj[:, head_width : 2 * head_width].astype(jnp.bfloat16)
    value_all = proj[:, 2 * head_width :].reshape(row_count, HEADS, ATT_EXP, HDIM)
    chosen = jnp.sum(
        (att_ids[..., None] == jnp.arange(ATT_EXP)[None, None, None, :]).astype(jnp.float32), axis=2
    )
    att_weight = jax.nn.sigmoid(att_logit.reshape(row_count, HEADS, ATT_EXP)) * chosen
    values = (
        jnp.sum(att_weight[..., None] * value_all, axis=2)
        .astype(jnp.bfloat16)
        .reshape(row_count, head_width)
    )
    first_row = lax.axis_index(("outer", "inner")) * row_count
    query_position = first_row + jnp.arange(row_count)
    score_factor = HDIM ** (-0.5)
    start_state = (
        jnp.full((row_count, HEADS), -1e30, jnp.float32),
        jnp.zeros((row_count, HEADS), jnp.float32),
        jnp.zeros((row_count, HEADS, HDIM), jnp.float32),
    )
    key_piece = lax.all_gather(keys, ("outer", "inner"), axis=0, tiled=True)
    value_piece = lax.all_gather(values, ("outer", "inner"), axis=0, tiled=True)
    piece_rows = key_piece.shape[0]

    def update(current):
        running_max, running_sum, accumulated = current
        key_heads = key_piece.reshape(piece_rows, HEADS, HDIM)
        value_heads = value_piece.reshape(piece_rows, HEADS, HDIM).astype(jnp.float32)
        scores = (
            jnp.einsum("thd,shd->ths", query, key_heads, preferred_element_type=jnp.float32)
            * score_factor
        )
        key_position = jnp.arange(piece_rows)
        visible = key_position[None, None, :] <= query_position[:, None, None]
        scores = jnp.where(visible, scores, -1e30)
        new_max = jnp.maximum(running_max, jnp.max(scores, axis=-1))
        weights = jnp.where(visible, jnp.exp(scores - new_max[..., None]), 0.0)
        new_sum = jnp.sum(weights, axis=-1)
        new_accum = jnp.einsum(
            "ths,shd->thd", weights, value_heads, precision=lax.Precision.HIGHEST
        )
        return (new_max, new_sum, new_accum)

    def keep_state(current):
        return current

    final_state = lax.cond(
        jnp.int32(0) <= first_row + row_count - 1, update, keep_state, start_state
    )
    attended = final_state[2] / final_state[1][..., None]
    head_normed = attended * lax.rsqrt(
        jnp.mean(attended * attended, axis=-1, keepdims=True) + epsilon
    )
    mixed = (head_normed[:, :, None, :] * att_weight[..., None]).reshape(
        row_count, HEADS * ATT_EXP * HDIM
    )
    mixed = mixed.astype(jnp.bfloat16)
    att_result = jnp.dot(
        mixed,
        lax.all_gather(att_out, "inner", axis=1, tiled=True),
        preferred_element_type=jnp.float32,
    )
    hidden_state = tokens.astype(jnp.float32) + att_result
    mlp_in = rms_norm(hidden_state, mlp_gain).astype(jnp.bfloat16)
    logits = jnp.dot(mlp_in, mlp_router, preferred_element_type=jnp.float32)
    expert_total = mlp_router.shape[1]
    picked = (mlp_ids[..., None] == jnp.arange(expert_total)[None, None, :]).astype(jnp.float32)
    gates = jax.nn.sigmoid(jnp.sum(picked * logits[:, None, :], axis=-1))
    outer_count = lax.axis_size("outer")
    inner_count = lax.axis_size("inner")
    device_count = outer_count * inner_count
    local_experts = w_up.shape[0]
    capacity = row_count * MLP_TOP * 5 // (4 * expert_total)
    flat_ids = mlp_ids.reshape(-1)
    one_hot = (flat_ids[:, None] == jnp.arange(expert_total)[None, :]).astype(jnp.int32)
    earlier = jnp.cumsum(one_hot, axis=0) - one_hot
    place_in_expert = jnp.sum(earlier * one_hot, axis=1)
    owner_device = flat_ids // local_experts
    owner_slot = flat_ids % local_experts
    slot_index = (owner_device * capacity + place_in_expert) * local_experts + owner_slot
    token_of_slot = jnp.full((device_count * capacity * local_experts,), row_count, jnp.int32)
    token_of_slot = token_of_slot.at[slot_index].set(jnp.arange(row_count * MLP_TOP) // MLP_TOP)
    padded_rows = jnp.concatenate([mlp_in, jnp.zeros((1, D), jnp.bfloat16)], axis=0)
    outgoing = padded_rows[token_of_slot].reshape(device_count, capacity, local_experts, D)
    hidden = jnp.einsum(
        "scej,ejh->sceh",
        lax.all_to_all(outgoing, ("outer", "inner"), split_axis=0, concat_axis=0, tiled=True),
        w_up,
        preferred_element_type=jnp.float32,
    )
    hidden = jnp.maximum(hidden, 0.0).astype(jnp.bfloat16)
    returned = lax.all_to_all(
        jnp.einsum("sceh,ehj->scej", hidden, w_down, preferred_element_type=jnp.float32).astype(
            jnp.bfloat16
        ),
        ("outer", "inner"),
        split_axis=0,
        concat_axis=0,
        tiled=True,
    )
    result_rows = returned.reshape(-1, D)[slot_index].reshape(row_count, MLP_TOP, D)
    mlp_out = jnp.sum(gates[..., None] * result_rows.astype(jnp.float32), axis=1)
    return (hidden_state + mlp_out).astype(jnp.bfloat16)


def solution(mesh):
    in_specs = (
        P(("seq", "outer", "inner"), None),
        P(("seq", "outer", "inner"), None, None),
        P(("seq", "outer", "inner"), None),
        P(),
        P("inner", None),
        P("inner", None),
        P(None, "inner"),
        P(),
        P(),
        P(("outer", "inner"), None, None),
        P(("outer", "inner"), None, None),
    )
    out_specs = P(("seq", "outer", "inner"), None)
    return jax.shard_map(
        on_device, mesh=mesh, in_specs=in_specs, out_specs=out_specs, check_vma=False
    )
```

profile of v0, /device:TPU:65, one launch (start us, length us, event | category | flops | bytes accessed | tf_op | source)
XLA Modules:
  0.0 937.8 jit_solution(16237632494527740651)
XLA Ops:
  6.5 0.7 all-gather.5.cloned.1.call-update
  7.3 1.5 fusion.14
  8.9 123.5 %all-gather.5.cloned.1.call-done = bf16[4096,768]{1,0:T(8,128)(2,1)} async-done(((bf16[1024,768]{1,0:T(8,128)(2,1)}), bf16[4096,768]{1,0:T(8,128)(2,1)}) %all-gather.5.cloned.1.call-update) | async-done | bytes 6291472 | tf_op jit(solution)/shard_map/all_gather | solution.py:41
  132.4 4.2 fusion.44
  136.6 0.6 slice.28
  137.3 10.8 %all_gather.17 = bf16[4096,8]{0,1:T(8,128)(2,1)S(1)} all-gather(bf16[1024,8]{0,1:T(8,128)(2,1)S(1)} %copy-done.8), channel_id=1, replica_groups=mesh['seq'=8,'outer'=8,'inner'=4] {'inner'}, dimensions={0}, use_global_device_ids=true | all-gather | bytes 81920 | tf_op jit(solution)/shard_map/all_gather | solution.py:46
  148.7 0.6 multiply_reduce_fusion.1
  150.4 18.0 %reduce-window.6 = s32[64,8,128]{2,1,0:T(8,128)S(1)} reduce-window(s32[64,8,128]{2,1,0:T(8,128)S(1)} %fusion.36, s32[]{:T(128)} %constant.87.clone.1), window={size=1x1x128 pad=0_0x0_0x127_0}, to_apply=%region_10.11 | reduce-window | flops 8323072 | bytes 524292 | tf_op jit(solution)/shard_map/reduce-window
  169.1 4.8 scatter_custom_fusion
  173.9 13.2 %all-gather.7.cloned.1.call-done = bf16[4096,128]{1,0:T(8,128)(2,1)} async-done(((bf16[128,128]{1,0:T(8,128)(2,1)}), bf16[4096,128]{1,0:T(8,128)(2,1)}) %all-gather.7.cloned.1.call-update) | async-done | bytes 1048592 | tf_op jit(solution)/shard_map/all_gather | solution.py:69
  187.1 52.0 %all-gather.9.cloned.1.call-done = bf16[4096,128]{0,1:T(8,128)(2,1)} async-done(((bf16[128,128]{0,1:T(8,128)(2,1)}), bf16[4096,128]{0,1:T(8,128)(2,1)}) %all-gather.9.cloned.1.call-update) | async-done | bytes 1048592 | tf_op jit(solution)/shard_map/all_gather | solution.py:70
  239.1 6.6 conditional.1
  239.6 1.5 copy.102
  241.1 1.2 fusion.43
  242.3 2.5 fusion.7
  244.8 0.8 fusion.3
  245.8 79.4 %all-gather.11.cloned.1.call-done = bf16[512,4096]{1,0:T(8,128)(2,1)} async-done(((bf16[512,1024]{1,0:T(8,128)(2,1)}), bf16[512,4096]{1,0:T(8,128)(2,1)}) %all-gather.11.cloned.1.call-update) | async-done | bytes 4194320 | tf_op jit(solution)/shard_map/all_gather | solution.py:108
  325.1 3.2 multiply_reduce_fusion
  328.3 1.3 copy-done.1
  329.9 1.0 copy-done.4
  331.0 8.4 gather_fusion
  339.4 17.4 %reshape.252 = bf16[32,20,2,4096]{3,2,1,0:T(2,128)(2,1)} reshape(bf16[1280,4096]{1,0:T(8,128)(2,1)} %gather_fusion) | data formatting | bytes 20971520 | tf_op jit(solution)/shard_map/reshape | solution.py:132
  356.8 238.7 %all_to_all.10 = bf16[32,20,2,4096]{3,2,1,0:T(2,128)(2,1)S(1)} all-to-all(bf16[32,20,2,4096]{3,2,1,0:T(2,128)(2,1)} %reshape.252), channel_id=1, replica_groups=mesh['seq'=8,'outer'=8,'inner'=4] {'outer','inner'}, dimensions={0} | all-to-all | bytes 20971520 | tf_op jit(solution)/shard_map/all_to_all | solution.py:135
  595.4 11.1 %fusion.21 = bf16[32,20,2,256]{3,1,0,2:T(8,128)(2,1)} fusion(bf16[2,4096,256]{2,1,0:T(8,128)(2,1)} %param.22, bf16[32,20,2,4096]{3,2,1,0:T(2,128)(2,1)S(1)} %all_to_all.10), kind=kOutput, calls=%fused_computation.34 | convolution fusion | flops 2685009920 | bytes 15335424 | tf_op jit(solution)/shard_map/scej,ejh->sceh/dot_general | solution.py:133
  606.5 5.3 convert_bitcast_fusion
  611.8 25.4 %copy.112 = bf16[32,20,2,4096]{3,2,1,0:T(2,128)(2,1)} copy(bf16[32,20,2,4096]{3,0,1,2:T(8,128)(2,1)S(1)} %convert_bitcast_fusion) | data formatting | bytes 20971520 | tf_op jit(solution)/shard_map/convert_element_type | solution.py:141
  637.2 6.7 all-to-all-start.1
  644.7 233.8 %all-to-all-done.1 = bf16[32,20,2,4096]{3,2,1,0:T(2,128)(2,1)} async-done(((bf16[32,20,2,4096]{3,2,1,0:T(2,128)(2,1)}), bf16[32,20,2,4096]{3,2,1,0:T(2,128)(2,1)}, u32[]{:S(2)}, u32[]{:S(2)}) %all-to-all-start.1) | async-done | bytes 10485792 | tf_op jit(solution)/shard_map/all_to_all | solution.py:140
  878.5 16.0 %reshape.253 = bf16[1280,4096]{1,0:T(8,128)(2,1)} reshape(bf16[32,20,2,4096]{3,2,1,0:T(2,128)(2,1)} %all-to-all-done.1) | data formatting | bytes 20971520 | tf_op jit(solution)/shard_map/reshape | solution.py:149
  894.6 20.4 %gather_fusion.1 = bf16[1024,4096]{1,0:T(8,128)(2,1)} fusion(bf16[1280,4096]{1,0:T(8,128)(2,1)} %reshape.253, s32[1024]{0:T(1024)S(1)} %broadcast_clamp_fusion), kind=kCustom, calls=%fused_computation.1 | custom fusion | bytes 16781312 | tf_op jit(solution)/shard_map/gather | solution.py:149
  914.9 13.3 %fusion.9 = f32[128,4096]{1,0:T(8,128)} fusion(bf16[1024,4096]{1,0:T(8,128)(2,1)} %gather_fusion.1, f32[128,8]{1,0:T(8,128)S(1)} %copy.104), kind=kLoop, calls=%fused_computation.18 | loop fusion | flops 12058624 | bytes 10489856 | tf_op jit(solution)/shard_map/reduce_sum | solution.py:150
  928.3 2.8 add_convert_fusion
  (69 shorter events, 4.1 us)
Async XLA Ops:
  6.5 637.5 %copy-start = (bf16[4096,64]{0,1:T(8,128)(2,1)S(1)}, bf16[4096,64]{0,1:T(8,128)(2,1)}, u32[]{:S(2)}) copy-start(bf16[4096,64]{0,1:T(8,128)(2,1)} %param.21) | copy-start | bytes 1572868
  6.5 125.8 %all-gather.5.cloned.1.call-start = ((), (), s32[]{:S(2)}) async-start(), calls=%async_computation.2 | async-start | bytes 7864320 | tf_op jit(solution)/shard_map/all_gather | solution.py:41
  7.3 179.8 %all-gather.7.cloned.1.call-start = ((), (), s32[]{:S(2)}) async-start(), calls=%async_computation.3 | async-start | bytes 1081344 | tf_op jit(solution)/shard_map/all_gather | solution.py:69
  8.8 128.4 %copy-start.8 = (bf16[1024,8]{0,1:T(8,128)(2,1)S(1)}, bf16[1024,8]{0,1:T(8,128)(2,1)}, u32[]{:S(2)}) copy-start(bf16[1024,8]{0,1:T(8,128)(2,1)} %param.18) | copy-start | bytes 49156
  8.8 139.2 %copy-start.10 = (s32[128,2,2]{0,2,1:T(2,128)S(1)}, s32[128,2,2]{0,2,1:T(2,128)}, u32[]{:S(2)}) copy-start(s32[128,2,2]{0,2,1:T(2,128)} %param.14) | copy-start | bytes 6148
  8.8 139.2 %copy-start.3 = (bf16[128,4096]{1,0:T(8,128)(2,1)S(1)}, bf16[128,4096]{1,0:T(8,128)(2,1)}, u32[]{:S(2)}) copy-start(bf16[128,4096]{1,0:T(8,128)(2,1)} %param.13) | copy-start | bytes 3145732
  8.9 139.2 %copy-start.6 = (f32[4096]{0:T(1024)S(1)}, f32[4096]{0:T(1024)}, u32[]{:S(2)}) copy-start(f32[4096]{0:T(1024)} %param.16) | copy-start | bytes 49156
  136.5 13.4 %copy-start.9 = (s32[128,8]{0,1:T(8,128)S(1)}, s32[128,8]{0,1:T(8,128)}, u32[]{:S(2)}) copy-start(s32[128,8]{0,1:T(8,128)} %param.15) | copy-start | bytes 12292
  137.2 101.9 %all-gather.9.cloned.1.call-start = ((), (), s32[]{:S(2)}) async-start(), calls=%async_computation.4 | async-start | bytes 1081344 | tf_op jit(solution)/shard_map/all_gather | solution.py:70
  149.4 175.8 %all-gather.11.cloned.1.call-start = ((), (), s32[]{:S(2)}) async-start(), calls=%async_computation.5 | async-start | bytes 5242880 | tf_op jit(solution)/shard_map/all_gather | solution.py:108
  241.1 1.2 copy-start.11
  325.1 4.5 copy-start.7
  328.3 1.3 copy-start.1
  329.9 1.0 copy-start.4
  637.2 6.8 copy-start.5
  637.2 241.3 %all-to-all-start.1 = ((bf16[32,20,2,4096]{3,2,1,0:T(2,128)(2,1)}), bf16[32,20,2,4096]{3,2,1,0:T(2,128)(2,1)}, u32[]{:S(2)}, u32[]{:S(2)}) async-start(bf16[32,20,2,4096]{3,2,1,0:T(2,128)(2,1)} %copy.112), calls=%async_computation.1 | async-start | bytes 20971520 | tf_op jit(solution)/shard_map/all_to_all | solution.py:140
  914.9 13.3 %copy-start.2 = (f32[128,4096]{1,0:T(8,128)S(1)}, f32[128,4096]{1,0:T(8,128)}, u32[]{:S(2)}) copy-start(f32[128,4096]{1,0:T(8,128)} %copy-done.1) | copy-start | bytes 6291460
Sparse Core Ops, SparseCore 0:
  9.2 123.1 all-gather.4
  137.3 49.7 all-gather.6
  189.5 49.4 all-gather.8
  240.7 84.3 all-gather.10
where the time goes:
time: 942 us; the launch traced here: 938 us
  waiting for transfers between devices  503 us (53%)
  blocking collectives  249 us (26%)
  local copies, waits for them, and re-layouts  98.1 us (10%)
  other arithmetic  38.2 us (4%)
  matrix products  28.3 us (3%)
  between operations  13.7 us (1%)
    all_to_all x1, blocking collectives, on_device(): lax.all_to_all(outgoing, ('outer', 'inner'), split_axis=0, concat_axis=0,...  239 us
    all_to_all x1, waiting for transfers between devices, on_device(): lax.all_to_all(jnp.einsum('sceh,ehj->scej', hidden, w_down, preferred_ele...  234 us
    all_gather x1, waiting for transfers between devices, on_device(): lax.all_gather(att_in, 'inner', axis=0, tiled=True)  123 us
    all_gather x1, waiting for transfers between devices, on_device(): lax.all_gather(att_out, 'inner', axis=1, tiled=True)  79.4 us
    all_gather x1, waiting for transfers between devices, on_device(): value_piece = lax.all_gather(values, ('outer', 'inner'), axis=0, tiled=True)  52 us
    convert_element_type x1, local copies, waits for them, and re-layouts, on_device(): jnp.einsum('sceh,ehj->scej', hidden, w_down, preferred_element_type=jnp.f...  25.4 us
    gather x1, local copies, waits for them, and re-layouts, on_device(): returned.reshape(-1, D)[slot_index].reshape(row_count, MLP_TOP, D)  20.4 us
  transfers between devices with their start and end apart: 5, of which 5 were waited for; matrix products, arithmetic and copies ran while one was open for 4% of the time, Pallas kernels for 0%

commit v1 on v0

--- a/solution.py
+++ b/solution.py
@@ -67,7 +67,17 @@
         jnp.zeros((row_count, HEADS, HDIM), jnp.float32),
     )
     key_piece = lax.all_gather(keys, ("outer", "inner"), axis=0, tiled=True)
-    value_piece = lax.all_gather(values, ("outer", "inner"), axis=0, tiled=True)
+
+    def place_terms_now(x0, d_out):
+        high = tuple((x0 for _ in range(lax.axis_size(("outer", "inner")))))
+        frame_out = jnp.stack(high, axis=0)
+        local_next = lax.all_to_all(
+            frame_out, axis_name=("outer", "inner"), split_axis=0, concat_axis=0
+        )
+        field_out = jnp.concatenate(local_next, d_out)
+        return field_out
+
+    value_piece = place_terms_now(values, 0)
     piece_rows = key_piece.shape[0]
 
     def update(current):

time: 942 us -> 900 us (0.955)
  waiting for transfers between devices: 503 us -> 445 us
  starting transfers between devices: 6.86 us -> 17.2 us
    all_gather x1 -> x0, waiting for transfers between devices: 52 us -> none  [on_device(): value_piece = lax.all_gather(values, ('outer', 'inner'), axis=0, tiled=True)]
    all_to_all x0 -> x1, starting transfers between devices: none -> 10.4 us  [place_terms_now(): lax.all_to_all(frame_out, axis_name=('outer', 'inner'), split_axis=0, con...]
  transfers between devices with their start and end apart: 5 -> 5, of which waited for: 5 -> 4; matrix products, arithmetic and copies ran while one was open for 4% -> 4% of each run, Pallas kernels for 0% -> 0%
where the time goes in v1:
time: 900 us; the launch traced here: 895 us
  waiting for transfers between devices  445 us (49%)
  blocking collectives  249 us (28%)
  local copies, waits for them, and re-layouts  103 us (11%)
  other arithmetic  37.6 us (4%)
  matrix products  28.4 us (3%)
  starting transfers between devices  17.2 us (2%)
  between operations  13.7 us (2%)
    all_to_all x1, blocking collectives, on_device(): lax.all_to_all(outgoing, ('outer', 'inner'), split_axis=0, concat_axis=0,...  239 us
    all_to_all x1, waiting for transfers between devices, on_device(): lax.all_to_all(jnp.einsum('sceh,ehj->scej', hidden, w_down, preferred_ele...  234 us
    all_gather x1, waiting for transfers between devices, on_device(): lax.all_gather(att_in, 'inner', axis=0, tiled=True)  123 us
    all_gather x1, waiting for transfers between devices, on_device(): lax.all_gather(att_out, 'inner', axis=1, tiled=True)  75.7 us
    convert_element_type x1, local copies, waits for them, and re-layouts, on_device(): jnp.einsum('sceh,ehj->scej', hidden, w_down, preferred_element_type=jnp.f...  25.4 us
    gather x1, local copies, waits for them, and re-layouts, on_device(): returned.reshape(-1, D)[slot_index].reshape(row_count, MLP_TOP, D)  20.4 us
    another operation x3, other arithmetic  18.2 us
  transfers between devices with their start and end apart: 5, of which 4 were waited for; matrix products, arithmetic and copies ran while one was open for 4% of the time, Pallas kernels for 0%

profile of v1, /device:TPU:65, one launch (start us, length us, event | category | flops | bytes accessed | tf_op | source)
XLA Modules:
  0.0 895.0 jit_solution(10702578713197618264)
XLA Ops:
  7.3 1.5 fusion.14
  8.9 123.5 %all-gather.4.cloned.1.call-done = bf16[4096,768]{1,0:T(8,128)(2,1)} async-done(((bf16[1024,768]{1,0:T(8,128)(2,1)}), bf16[4096,768]{1,0:T(8,128)(2,1)}) %all-gather.4.cloned.1.call-update) | async-done | bytes 6291472 | tf_op jit(solution)/shard_map/all_gather | solution.py:41
  132.4 4.2 fusion.44
  137.9 10.8 %all_gather.14 = bf16[4096,8]{0,1:T(8,128)(2,1)S(1)} all-gather(bf16[1024,8]{0,1:T(8,128)(2,1)S(1)} %copy-done.9), channel_id=1, replica_groups=mesh['seq'=8,'outer'=8,'inner'=4] {'inner'}, dimensions={0}, use_global_device_ids=true | all-gather | bytes 81920 | tf_op jit(solution)/shard_map/all_gather | solution.py:46
  149.4 1.2 stack.3
  150.6 10.4 %all-to-all-start = ((bf16[32,128,128]{1,2,0:T(8,128)(2,1)}), bf16[32,128,128]{1,2,0:T(8,128)(2,1)S(1)}, u32[]{:S(2)}, u32[]{:S(2)}) async-start(bf16[32,128,128]{1,2,0:T(8,128)(2,1)} %stack.3), calls=%async_computation | async-start | bytes 2097152 | tf_op jit(solution)/shard_map/all_to_all | solution.py:74
  161.4 18.0 %reduce-window.6 = s32[64,8,128]{2,1,0:T(8,128)S(1)} reduce-window(s32[64,8,128]{2,1,0:T(8,128)S(1)} %fusion.36, s32[]{:T(128)} %constant.87.clone.1), window={size=1x1x128 pad=0_0x0_0x127_0}, to_apply=%region_10.11 | reduce-window | flops 8323072 | bytes 524292 | tf_op jit(solution)/shard_map/reduce-window
  180.1 4.8 scatter_custom_fusion
  184.9 11.0 %all-gather.6.cloned.1.call-done = bf16[4096,128]{1,0:T(8,128)(2,1)} async-done(((bf16[128,128]{1,0:T(8,128)(2,1)}), bf16[4096,128]{1,0:T(8,128)(2,1)}) %all-gather.6.cloned.1.call-update) | async-done | bytes 1048592 | tf_op jit(solution)/shard_map/all_gather | solution.py:69
  195.9 10.5 %conditional.1 = (f32[128,2]{0,1:T(2,128)S(1)}, f32[128,2,64]{0,2,1:T(8,128)S(1)}) conditional(s32[]{:T(128)} %convert_element_type.63, () %tuple.13, (s32[]{:T(128)}, s32[128]{0:T(128)S(1)}, bf16[4096,128]{1,0:T(8,128)(2,1)}, bf16[128,768]{1,0:T(8,128)(2,1)S(1)}, bf16[32,128,128]{1,2,0:T(8,128)(2,1)S(1)}) %tuple.14), branch_computations={%region_3.0_spmd, %region_4.7_spmd} | conditional | flops 948436864 | bytes 27827760 | solution.py:105
  195.9 1.6 copy.108
  197.6 2.3 reshape_reshape.2
  200.4 1.5 copy.106
  201.9 1.2 fusion.43
  203.2 2.5 fusion.7
  205.6 0.8 fusion.3
  206.6 75.7 %all-gather.8.cloned.1.call-done = bf16[512,4096]{1,0:T(8,128)(2,1)} async-done(((bf16[512,1024]{1,0:T(8,128)(2,1)}), bf16[512,4096]{1,0:T(8,128)(2,1)}) %all-gather.8.cloned.1.call-update) | async-done | bytes 4194320 | tf_op jit(solution)/shard_map/all_gather | solution.py:118
  282.3 3.2 multiply_reduce_fusion
  285.5 1.3 copy-done.1
  287.1 1.0 copy-done.4
  288.2 8.4 gather_fusion
  296.6 17.4 %reshape.250 = bf16[32,20,2,4096]{3,2,1,0:T(2,128)(2,1)} reshape(bf16[1280,4096]{1,0:T(8,128)(2,1)} %gather_fusion) | data formatting | bytes 20971520 | tf_op jit(solution)/shard_map/reshape | solution.py:142
  314.0 238.7 %all_to_all.15 = bf16[32,20,2,4096]{3,2,1,0:T(2,128)(2,1)S(1)} all-to-all(bf16[32,20,2,4096]{3,2,1,0:T(2,128)(2,1)} %reshape.250), channel_id=1, replica_groups=mesh['seq'=8,'outer'=8,'inner'=4] {'outer','inner'}, dimensions={0} | all-to-all | bytes 20971520 | tf_op jit(solution)/shard_map/all_to_all | solution.py:145
  552.6 11.1 %fusion.21 = bf16[32,20,2,256]{3,1,0,2:T(8,128)(2,1)} fusion(bf16[2,4096,256]{2,1,0:T(8,128)(2,1)} %param.22, bf16[32,20,2,4096]{3,2,1,0:T(2,128)(2,1)S(1)} %all_to_all.15), kind=kOutput, calls=%fused_computation.34 | convolution fusion | flops 2685009920 | bytes 15335424 | tf_op jit(solution)/shard_map/scej,ejh->sceh/dot_general | solution.py:143
  563.7 5.3 convert_bitcast_fusion
  569.0 25.4 %copy.117 = bf16[32,20,2,4096]{3,2,1,0:T(2,128)(2,1)} copy(bf16[32,20,2,4096]{3,0,1,2:T(8,128)(2,1)S(1)} %convert_bitcast_fusion) | data formatting | bytes 20971520 | tf_op jit(solution)/shard_map/convert_element_type | solution.py:151
  594.4 6.7 all-to-all-start.2
  601.9 233.8 %all-to-all-done.2 = bf16[32,20,2,4096]{3,2,1,0:T(2,128)(2,1)} async-done(((bf16[32,20,2,4096]{3,2,1,0:T(2,128)(2,1)}), bf16[32,20,2,4096]{3,2,1,0:T(2,128)(2,1)}, u32[]{:S(2)}, u32[]{:S(2)}) %all-to-all-start.2) | async-done | bytes 10485792 | tf_op jit(solution)/shard_map/all_to_all | solution.py:150
  835.7 16.0 %reshape.251 = bf16[1280,4096]{1,0:T(8,128)(2,1)} reshape(bf16[32,20,2,4096]{3,2,1,0:T(2,128)(2,1)} %all-to-all-done.2) | data formatting | bytes 20971520 | tf_op jit(solution)/shard_map/reshape | solution.py:159
  851.7 20.4 %gather_fusion.1 = bf16[1024,4096]{1,0:T(8,128)(2,1)} fusion(bf16[1280,4096]{1,0:T(8,128)(2,1)} %reshape.251, s32[1024]{0:T(1024)S(1)} %broadcast_clamp_fusion), kind=kCustom, calls=%fused_computation.1 | custom fusion | bytes 16781312 | tf_op jit(solution)/shard_map/gather | solution.py:159
  872.1 13.3 %fusion.9 = f32[128,4096]{1,0:T(8,128)} fusion(bf16[1024,4096]{1,0:T(8,128)(2,1)} %gather_fusion.1, f32[128,8]{1,0:T(8,128)S(1)} %copy.109), kind=kLoop, calls=%fused_computation.18 | loop fusion | flops 12058624 | bytes 10489856 | tf_op jit(solution)/shard_map/reduce_sum | solution.py:160
  885.5 2.8 add_convert_fusion
  (71 shorter events, 5.5 us)
Async XLA Ops:
  6.5 594.7 %copy-start = (bf16[4096,64]{0,1:T(8,128)(2,1)S(1)}, bf16[4096,64]{0,1:T(8,128)(2,1)}, u32[]{:S(2)}) copy-start(bf16[4096,64]{0,1:T(8,128)(2,1)} %param.21) | copy-start | bytes 1572868
  6.5 125.8 %all-gather.4.cloned.1.call-start = ((), (), s32[]{:S(2)}) async-start(), calls=%async_computation.3 | async-start | bytes 7864320 | tf_op jit(solution)/shard_map/all_gather | solution.py:41
  7.3 188.7 %all-gather.6.cloned.1.call-start = ((), (), s32[]{:S(2)}) async-start(), calls=%async_computation.4 | async-start | bytes 1081344 | tf_op jit(solution)/shard_map/all_gather | solution.py:69
  8.8 129.1 %copy-start.9 = (bf16[1024,8]{0,1:T(8,128)(2,1)S(1)}, bf16[1024,8]{0,1:T(8,128)(2,1)}, u32[]{:S(2)}) copy-start(bf16[1024,8]{0,1:T(8,128)(2,1)} %param.18) | copy-start | bytes 49156
  8.8 139.9 %copy-start.11 = (s32[128,2,2]{0,2,1:T(2,128)S(1)}, s32[128,2,2]{0,2,1:T(2,128)}, u32[]{:S(2)}) copy-start(s32[128,2,2]{0,2,1:T(2,128)} %param.14) | copy-start | bytes 6148
  8.9 139.9 %copy-start.3 = (bf16[128,4096]{1,0:T(8,128)(2,1)S(1)}, bf16[128,4096]{1,0:T(8,128)(2,1)}, u32[]{:S(2)}) copy-start(bf16[128,4096]{1,0:T(8,128)(2,1)} %param.13) | copy-start | bytes 3145732
  8.9 139.9 %copy-start.7 = (f32[4096]{0:T(1024)S(1)}, f32[4096]{0:T(1024)}, u32[]{:S(2)}) copy-start(f32[4096]{0:T(1024)} %param.16) | copy-start | bytes 49156
  136.5 24.4 %copy-start.10 = (s32[128,8]{0,1:T(8,128)S(1)}, s32[128,8]{0,1:T(8,128)}, u32[]{:S(2)}) copy-start(s32[128,8]{0,1:T(8,128)} %param.15) | copy-start | bytes 12292
  137.2 145.1 %all-gather.8.cloned.1.call-start = ((), (), s32[]{:S(2)}) async-start(), calls=%async_computation.5 | async-start | bytes 5242880 | tf_op jit(solution)/shard_map/all_gather | solution.py:118
  150.6 45.3 %all-to-all-start = ((bf16[32,128,128]{1,2,0:T(8,128)(2,1)}), bf16[32,128,128]{1,2,0:T(8,128)(2,1)S(1)}, u32[]{:S(2)}, u32[]{:S(2)}) async-start(bf16[32,128,128]{1,2,0:T(8,128)(2,1)} %stack.3), calls=%async_computation | async-start | bytes 2097152 | tf_op jit(solution)/shard_map/all_to_all | solution.py:74
  201.9 1.2 copy-start.6
  282.3 4.5 copy-start.8
  285.5 1.3 copy-start.1
  287.1 1.0 copy-start.4
  594.4 6.8 copy-start.5
  594.4 241.3 %all-to-all-start.2 = ((bf16[32,20,2,4096]{3,2,1,0:T(2,128)(2,1)}), bf16[32,20,2,4096]{3,2,1,0:T(2,128)(2,1)}, u32[]{:S(2)}, u32[]{:S(2)}) async-start(bf16[32,20,2,4096]{3,2,1,0:T(2,128)(2,1)} %copy.117), calls=%async_computation.2 | async-start | bytes 20971520 | tf_op jit(solution)/shard_map/all_to_all | solution.py:150
  872.1 13.3 %copy-start.2 = (f32[128,4096]{1,0:T(8,128)S(1)}, f32[128,4096]{1,0:T(8,128)}, u32[]{:S(2)}) copy-start(f32[128,4096]{1,0:T(8,128)} %copy-done.1) | copy-start | bytes 6291460
Sparse Core Ops, SparseCore 0:
  9.2 123.1 all-gather.3
  137.3 58.5 all-gather.5
  197.7 84.5 all-gather.7
